TPU v7x, 256 devices: a whole 4x4x8 slice. The times are simulated.
256 devices in a mesh: rows: 32 (over y, z), tensor: 8 (over x, core).
Axes of the slice: x: 4, y: 4, z: 8, core: 2. Of those that a mesh axis runs over, the one named last changes fastest.
Arguments:
- token_ids: int32 [256, 4], replicated, may hold values from 0 to 65535
- cache_lengths: int32 [256], P('rows'), may hold values from 160 to 1280, as said below
- doc_ids: int32 [256], replicated, may hold values from 0 to 31
- embed_table: bfloat16 [65536, 8192], P('tensor', 'rows'), may hold values from -10.5 to 10.5
- cache_keys: bfloat16 [256, 1280, 1024], P('rows', None, 'tensor'), may hold values from -700 to 700
- cache_values: bfloat16 [256, 1280, 1024], P('rows', None, 'tensor'), may hold values from -6 to 6
- decode_gain: float32 [8192], P('rows'), may hold values from 0.1 to 1.9
- decode_query: bfloat16 [8192, 8192], P('rows', 'tensor'), may hold values from -0.0625 to 0.0625
- decode_key: bfloat16 [8192, 1024], P('rows', 'tensor'), may hold values from -0.0625 to 0.0625
- decode_value: bfloat16 [8192, 1024], P('rows', 'tensor'), may hold values from -0.0625 to 0.0625
- decode_out: bfloat16 [8192, 8192], P('tensor', 'rows'), may hold values from -0.0625 to 0.0625
- reduce_gain: float32 [8192], P('rows'), may hold values from 0.8 to 10
- reduce_query: bfloat16 [8192, 8192], P('rows', 'tensor'), may hold values from -0.0625 to 0.0625
- reduce_key: bfloat16 [8192, 1024], P('rows', 'tensor'), may hold values from -0.0625 to 0.0625
- reduce_value: bfloat16 [8192, 1024], P('rows', 'tensor'), may hold values from -0.0625 to 0.0625
- reduce_out: bfloat16 [8192, 8192], P('tensor', 'rows'), may hold values from -0.0625 to 0.0625
Outputs:
- reduced: bfloat16 [1024, 8192], P(None, 'rows')
Inputs may be any that keep to these rules, and one draw needn't show every extreme that they name: Passage row c holds cache entries at positions below cache_lengths[c]; one row in every draw has a full cache of 1280.
All inputs are finite; a program needn't handle non-finite values.
Results may differ from a plain program's by a relative error of at most 0.035.
The roundings to bfloat16 on the way count: a program that leaves them out, or rounds other values in their place, can miss the bound.
Values may be sent and summed in bfloat16 or wider, within the bound.
A program may use at most 64 MiB of HBM per device.

v0:
```python
import jax
import jax.numpy as jnp
from jax import lax
from jax.sharding import PartitionSpec as P

D = 8192
HEAD_DIM = 128


EPSILON = 1e-05
ROPE_BASE = 500000.0


def rotate(vectors, positions):
    half_dim = vectors.shape[-1] // 2
    frequencies = ROPE_BASE ** (-2.0 * jnp.arange(half_dim, dtype=jnp.float32) / vectors.shape[-1])
    angles = positions.astype(jnp.float32)[..., None] * frequencies
    cosine = jnp.cos(angles)
    sine_part = jnp.sin(angles)
    lower_half = vectors[..., :half_dim]
    upper_half = vectors[..., half_dim:]
    return jnp.concatenate(
        [
            lower_half * cosine - upper_half * sine_part,
            upper_half * cosine + lower_half * sine_part,
        ],
        axis=-1,
    )


def width_total(partial_value):
    return lax.psum(partial_value, "tensor")


def row_scale(squares):
    summed = lax.psum(squares, "rows")
    return lax.rsqrt(summed / D + EPSILON)


def head_terms(normed, matrices):
    return lax.psum_scatter(
        jnp.concatenate(
            [jnp.dot(normed, matrix, preferred_element_type=jnp.float32) for matrix in matrices],
            axis=1,
        ),
        "rows",
        scatter_dimension=0,
        tiled=True,
    )


def head_mix(attended, matrix):
    return jnp.dot(
        lax.all_gather(attended, "rows", axis=0, tiled=True),
        matrix,
        preferred_element_type=jnp.float32,
    )


def per_device(
    token_ids,
    cache_lengths,
    doc_ids,
    embed_table,
    cache_keys,
    cache_values,
    decode_gain,
    decode_query,
    decode_key,
    decode_value,
    decode_out,
    reduce_gain,
    reduce_query,
    reduce_key,
    reduce_value,
    reduce_out,
):
    step_count = token_ids.shape[1]
    passage_count = token_ids.shape[0]
    token_count = passage_count * step_count
    own_passages = cache_lengths.shape[0]
    own_tokens = own_passages * step_count
    row_first = lax.axis_index("rows") * own_tokens
    query_cols = decode_query.shape[1]
    kv_cols = decode_key.shape[1]
    local_heads = query_cols // HEAD_DIM
    local_kv = kv_cols // HEAD_DIM
    group_size = local_heads // local_kv
    score_scale = HEAD_DIM ** (-0.5)
    step_ids = jnp.arange(step_count, dtype=jnp.int32)
    vocab_part = embed_table.shape[0]
    local_ids = token_ids.reshape(token_count) - lax.axis_index("tensor") * vocab_part
    inside = (local_ids >= 0) & (local_ids < vocab_part)
    picked = jnp.take(embed_table, jnp.clip(local_ids, 0, vocab_part - 1), axis=0)
    picked = jnp.where(inside[:, None], picked.astype(jnp.float32), 0.0)
    embedded = width_total(picked)
    dec_scale = row_scale(jnp.sum(embedded * embedded, axis=1))
    normed = (embedded * decode_gain[None, :]).astype(jnp.bfloat16)
    projected = head_terms(normed, (decode_query, decode_key, decode_value))
    projected = projected * lax.dynamic_slice_in_dim(dec_scale, row_first, own_tokens, 0)[:, None]
    positions = (cache_lengths[:, None] + step_ids[None, :]).reshape(own_tokens, 1)
    queries = rotate(
        projected[:, :query_cols].reshape(own_tokens, local_heads, HEAD_DIM), positions
    ).astype(jnp.bfloat16)
    keys_new = rotate(
        projected[:, query_cols : query_cols + kv_cols].reshape(own_tokens, local_kv, HEAD_DIM),
        positions,
    ).astype(jnp.bfloat16)
    values_new = projected[:, query_cols + kv_cols :].astype(jnp.bfloat16)
    queries = queries.reshape(own_passages, step_count, local_kv, group_size, HEAD_DIM)
    keys_new = keys_new.reshape(own_passages, step_count, local_kv, HEAD_DIM)
    values_new = values_new.reshape(own_passages, step_count, local_kv, HEAD_DIM)
    capacity = cache_keys.shape[1]
    keys_old = cache_keys.reshape(own_passages, capacity, local_kv, HEAD_DIM)
    values_old = cache_values.reshape(own_passages, capacity, local_kv, HEAD_DIM)
    new_scores = (
        jnp.einsum("rskgd,rtkd->rskgt", queries, keys_new, preferred_element_type=jnp.float32)
        * score_scale
    )
    causal = step_ids[None, :] <= step_ids[:, None]
    new_scores = jnp.where(causal[None, :, None, None, :], new_scores, -jnp.inf)
    old_scores = (
        jnp.einsum("rskgd,rckd->rskgc", queries, keys_old, preferred_element_type=jnp.float32)
        * score_scale
    )
    slot_ids = jnp.arange(capacity, dtype=jnp.int32)
    live_mask = slot_ids[None, :] < cache_lengths[:, None]
    old_scores = jnp.where(live_mask[:, None, None, None, :], old_scores, -jnp.inf)
    highest = jnp.maximum(jnp.max(old_scores, axis=-1), jnp.max(new_scores, axis=-1))
    old_exp = jnp.exp(old_scores - highest[..., None])
    new_exp = jnp.exp(new_scores - highest[..., None])
    summed = jnp.sum(old_exp, axis=-1) + jnp.sum(new_exp, axis=-1)
    old_weights = (old_exp / summed[..., None]).astype(jnp.bfloat16)
    new_weights = (new_exp / summed[..., None]).astype(jnp.bfloat16)
    attended = jnp.einsum(
        "rskgc,rckd->rskgd", old_weights, values_old, preferred_element_type=jnp.float32
    )
    attended = attended + jnp.einsum(
        "rskgt,rtkd->rskgd", new_weights, values_new, preferred_element_type=jnp.float32
    )
    attended = attended.reshape(own_tokens, query_cols).astype(jnp.bfloat16)
    partial_value = head_mix(attended, decode_out)
    summary = (embedded + width_total(partial_value)).astype(jnp.bfloat16)
    summary_wide = summary.astype(jnp.float32)
    red_scale = row_scale(jnp.sum(summary_wide * summary_wide, axis=1))
    normed_red = (summary_wide * reduce_gain[None, :]).astype(jnp.bfloat16)
    passage_index = jnp.arange(passage_count, dtype=jnp.int32)
    earlier = jnp.sum(
        (
            (doc_ids[None, :] == doc_ids[:, None])
            & (passage_index[None, :] < passage_index[:, None])
        ).astype(jnp.int32),
        axis=1,
    )
    doc_positions = (earlier[:, None] * step_count + step_ids[None, :]).reshape(token_count, 1)
    doc_tokens = (doc_ids[:, None] + jnp.zeros_like(step_ids)[None, :]).reshape(token_count)
    own_positions = lax.dynamic_slice_in_dim(doc_positions, row_first, own_tokens, 0)
    own_scale = lax.dynamic_slice_in_dim(red_scale, row_first, own_tokens, 0)[:, None]
    projected = head_terms(normed_red, (reduce_query, reduce_key, reduce_value)) * own_scale
    queries_red = rotate(
        projected[:, :query_cols].reshape(own_tokens, local_heads, HEAD_DIM), own_positions
    ).astype(jnp.bfloat16)
    keys_own = (
        rotate(
            projected[:, query_cols : query_cols + kv_cols].reshape(own_tokens, local_kv, HEAD_DIM),
            own_positions,
        )
        .astype(jnp.bfloat16)
        .reshape(own_tokens, kv_cols)
    )
    values_own = projected[:, query_cols + kv_cols :].astype(jnp.bfloat16)
    keys_red, values_red = (
        lax.all_gather(keys_own, "rows", axis=0, tiled=True),
        lax.all_gather(values_own, "rows", axis=0, tiled=True),
    )
    queries_red = queries_red.reshape(own_tokens, local_kv, group_size, HEAD_DIM)
    keys_red = keys_red.reshape(token_count, local_kv, HEAD_DIM)
    values_red = values_red.reshape(token_count, local_kv, HEAD_DIM)
    token_index = jnp.arange(token_count, dtype=jnp.int32)
    own_index = row_first + jnp.arange(own_tokens, dtype=jnp.int32)
    own_docs = lax.dynamic_slice_in_dim(doc_tokens, row_first, own_tokens, 0)
    allowed = (own_docs[:, None] == doc_tokens[None, :]) & (
        token_index[None, :] <= own_index[:, None]
    )
    red_scores = (
        jnp.einsum("tkgd,ukd->tkgu", queries_red, keys_red, preferred_element_type=jnp.float32)
        * score_scale
    )
    red_scores = jnp.where(allowed[:, None, None, :], red_scores, -jnp.inf)
    red_high = jnp.max(red_scores, axis=-1)
    red_exp = jnp.exp(red_scores - red_high[..., None])
    red_weights = (red_exp / jnp.sum(red_exp, axis=-1)[..., None]).astype(jnp.bfloat16)
    red_out = jnp.einsum(
        "tkgu,ukd->tkgd", red_weights, values_red, preferred_element_type=jnp.float32
    )
    red_out = red_out.reshape(own_tokens, query_cols).astype(jnp.bfloat16)
    return (summary_wide + width_total(head_mix(red_out, reduce_out))).astype(jnp.bfloat16)


def solution(mesh):
    return jax.shard_map(
        per_device,
        mesh=mesh,
        in_specs=(
            P(),
            P("rows"),
            P(),
            P("tensor", "rows"),
            P("rows", None, "tensor"),
            P("rows", None, "tensor"),
            P("rows"),
            P("rows", "tensor"),
            P("rows", "tensor"),
            P("rows", "tensor"),
            P("tensor", "rows"),
            P("rows"),
            P("rows", "tensor"),
            P("rows", "tensor"),
            P("rows", "tensor"),
            P("tensor", "rows"),
        ),
        out_specs=P(None, "rows"),
        check_vma=False,
    )
```

profile of v0, /device:TPU:8, one launch (start us, length us, event | category | flops | bytes accessed | tf_op | source)
XLA Modules:
  0.0 966.4 jit_solution(12764112662389864731)
XLA Ops:
  8.8 6.2 gather_fusion
  15.0 1.3 convert_select_fusion
  16.4 70.6 %all-reduce.4.cloned.1.call-done = f32[1024,256]{1,0:T(8,128)} async-done(((f32[1024,256]{1,0:T(8,128)}), f32[1024,256]{1,0:T(8,128)}) %all-reduce.4.cloned.1.call-update) | async-done | bytes 1048592 | tf_op jit(solution)/shard_map/psum | solution.py:32
  87.1 1.4 multiply_reduce_fusion
  90.0 2.8 pad_maximum_fusion
  92.8 5.9 copy.69
  100.4 63.5 %psum.36 = f32[1024]{0:T(1024)S(1)} all-reduce(f32[1024]{0:T(1024)S(1)} %get-tuple-element.7), channel_id=1, replica_groups=mesh['rows'=32,'tensor'=8] {'rows'}, use_global_device_ids=true, to_apply=%region_3.4 | all-reduce | flops 1024 | bytes 8192 | tf_op jit(solution)/shard_map/psum | solution.py:36
  164.0 160.3 %reduce-scatter.7.cloned.1.call-done = f32[32,1280]{1,0:T(8,128)} async-done(((f32[1024,1280]{1,0:T(8,128)}), f32[32,1280]{1,0:T(8,128)}) %reduce-scatter.7.cloned.1.call-update) | async-done | bytes 163856 | tf_op jit(solution)/shard_map/reduce_scatter | solution.py:41
  325.6 1.1 fusion.69
  329.2 75.8 %all-gather.3.cloned.1.call-done = bf16[1024,1024]{1,0:T(8,128)(2,1)} async-done(((bf16[32,1024]{1,0:T(8,128)(2,1)}), bf16[1024,1024]{1,0:T(8,128)(2,1)}) %all-gather.3.cloned.1.call-update) | async-done | bytes 2097168 | tf_op jit(solution)/shard_map/all_gather | solution.py:54
  405.0 3.3 fusion.75
  408.3 66.2 %all-reduce.6.cloned.1.call-done = f32[1024,256]{1,0:T(8,128)} async-done(((f32[1024,256]{1,0:T(8,128)}), f32[1024,256]{1,0:T(8,128)}) %all-reduce.6.cloned.1.call-update) | async-done | bytes 1048592 | tf_op jit(solution)/shard_map/psum | solution.py:32
  474.6 1.8 fusion.22
  476.4 1.8 fusion.32
  478.9 2.8 pad_maximum_fusion.1
  481.6 5.9 copy.71
  488.0 63.5 %psum.38 = f32[1024]{0:T(1024)S(1)} all-reduce(f32[1024]{0:T(1024)S(1)} %get-tuple-element.5), channel_id=1, replica_groups=mesh['rows'=32,'tensor'=8] {'rows'}, use_global_device_ids=true, to_apply=%region_11.12 | all-reduce | flops 1024 | bytes 8192 | tf_op jit(solution)/shard_map/psum | solution.py:36
  551.7 161.6 %reduce-scatter.9.cloned.1.call-done = f32[32,1280]{1,0:T(8,128)} async-done(((f32[1024,1280]{1,0:T(8,128)}), f32[32,1280]{1,0:T(8,128)}) %reduce-scatter.9.cloned.1.call-update) | async-done | bytes 163856 | tf_op jit(solution)/shard_map/reduce_scatter | solution.py:41
  714.5 47.5 %all_gather.14 = bf16[1024,128]{1,0:T(8,128)(2,1)S(1)} all-gather(bf16[32,128]{1,0:T(8,128)(2,1)S(1)} %pad_maximum_fusion.5), channel_id=1, replica_groups=mesh['rows'=32,'tensor'=8] {'rows'}, dimensions={0}, use_global_device_ids=true | all-gather | bytes 270336 | tf_op jit(solution)/shard_map/all_gather | solution.py:173
  762.1 47.8 %all_gather.13 = bf16[1024,128]{1,0:T(8,128)(2,1)S(1)} all-gather(bf16[32,128]{1,0:T(8,128)(2,1)S(1)} %slice.100), channel_id=1, replica_groups=mesh['rows'=32,'tensor'=8] {'rows'}, dimensions={0}, use_global_device_ids=true | all-gather | bytes 270336 | tf_op jit(solution)/shard_map/all_gather | solution.py:174
  811.9 75.9 %all-gather.5.cloned.1.call-done = bf16[1024,1024]{1,0:T(8,128)(2,1)} async-done(((bf16[32,1024]{1,0:T(8,128)(2,1)}), bf16[1024,1024]{1,0:T(8,128)(2,1)}) %all-gather.5.cloned.1.call-update) | async-done | bytes 2097168 | tf_op jit(solution)/shard_map/all_gather | solution.py:54
  887.7 3.4 fusion.76
  891.1 66.3 %all-reduce.8.cloned.1.call-done = f32[1024,256]{1,0:T(8,128)} async-done(((f32[1024,256]{1,0:T(8,128)}), f32[1024,256]{1,0:T(8,128)}) %all-reduce.8.cloned.1.call-update) | async-done | bytes 1048592 | tf_op jit(solution)/shard_map/psum | solution.py:32
  957.4 2.1 fusion.23
  (102 shorter events, 13.6 us)
Async XLA Ops:
  6.5 319.0 %copy-start = (bf16[8,1280,128]{2,1,0:T(8,128)(2,1)S(1)}, bf16[8,1280,128]{2,1,0:T(8,128)(2,1)}, u32[]{:S(2)}) copy-start(bf16[8,1280,128]{2,1,0:T(8,128)(2,1)} %param.20) | copy-start | bytes 7864324
  6.5 80.5 %all-reduce.4.cloned.1.call-start = ((), (), s32[]{:S(2)}) async-start(), calls=%async_computation.2 | async-start | bytes 2097152 | tf_op jit(solution)/shard_map/psum | solution.py:32
  8.8 78.3 %copy-start.9 = (f32[256]{0:T(256)S(1)}, f32[256]{0:T(256)}, u32[]{:S(2)}) copy-start(f32[256]{0:T(256)} %param.22) | copy-start | bytes 3076
  16.4 72.2 %copy-start.1 = (bf16[256,1024]{1,0:T(8,128)(2,1)S(1)}, bf16[256,1024]{1,0:T(8,128)(2,1)}, u32[]{:S(2)}) copy-start(bf16[256,1024]{1,0:T(8,128)(2,1)} %param.23) | copy-start | bytes 1572868
  16.4 307.8 %reduce-scatter.7.cloned.1.call-start = ((), (), s32[]{:S(2)}) async-start(), calls=%async_computation.7 | async-start | bytes 5406720 | tf_op jit(solution)/shard_map/reduce_scatter | solution.py:41
  88.5 0.8 copy-start.2
  88.5 1.1 copy-start.3
  98.7 0.7 copy-start.7
  98.7 1.1 copy-start.8
  98.8 306.2 %all-gather.3.cloned.1.call-start = ((), (), s32[]{:S(2)}) async-start(), calls=%async_computation.3 | async-start | bytes 2162688 | tf_op jit(solution)/shard_map/all_gather | solution.py:54
  325.6 2.3 copy-start.10
  327.9 77.1 %copy-start.11 = (bf16[1024,256]{1,0:T(8,128)(2,1)S(1)}, bf16[1024,256]{1,0:T(8,128)(2,1)}, u32[]{:S(2)}) copy-start(bf16[1024,256]{1,0:T(8,128)(2,1)} %param.26) | copy-start | bytes 1572868
  329.1 145.4 %all-reduce.6.cloned.1.call-start = ((), (), s32[]{:S(2)}) async-start(), calls=%async_computation.4 | async-start | bytes 2097152 | tf_op jit(solution)/shard_map/psum | solution.py:32
  408.3 68.1 %copy-start.6 = (f32[256]{0:T(256)S(1)}, f32[256]{0:T(256)}, u32[]{:S(2)}) copy-start(f32[256]{0:T(256)} %param.27) | copy-start | bytes 3076
  408.3 305.0 %reduce-scatter.9.cloned.1.call-start = ((), (), s32[]{:S(2)}) async-start(), calls=%async_computation.8 | async-start | bytes 5406720 | tf_op jit(solution)/shard_map/reduce_scatter | solution.py:41
  476.3 1.9 copy-start.4
  476.3 2.2 copy-start.5
  487.6 400.1 %all-gather.5.cloned.1.call-start = ((), (), s32[]{:S(2)}) async-start(), calls=%async_computation.5 | async-start | bytes 2162688 | tf_op jit(solution)/shard_map/all_gather | solution.py:54
  811.8 145.6 %all-reduce.8.cloned.1.call-start = ((), (), s32[]{:S(2)}) async-start(), calls=%async_computation.6 | async-start | bytes 2097152 | tf_op jit(solution)/shard_map/psum | solution.py:32
Sparse Core Ops, SparseCore 0:
  16.5 70.5 all-reduce.3
  98.9 225.3 reduce-scatter.6
  329.3 75.6 all-gather.2
  408.4 66.1 all-reduce.5
  487.7 225.4 reduce-scatter.8
  811.9 75.7 all-gather.4
  891.3 66.1 all-reduce.7
where the time goes:
time: 967 us; the launch traced here: 966 us
  waiting for transfers between devices  677 us (70%)
  blocking collectives  222 us (23%)
  local copies, waits for them, and re-layouts  21.6 us (2%)
  other arithmetic  17.9 us (2%)
  between operations  13.9 us (1%)
  matrix products  13.7 us (1%)
    reduce_scatter x2, waiting for transfers between devices, head_terms(): lax.psum_scatter(jnp.concatenate([jnp.dot(normed, matrix, preferred_eleme...  322 us
    psum x3, waiting for transfers between devices, width_total(): return lax.psum(partial_value, 'tensor')  203 us
    all_gather x2, waiting for transfers between devices, head_mix(): lax.all_gather(attended, 'rows', axis=0, tiled=True)  152 us
    psum x2, blocking collectives, row_scale(): summed = lax.psum(squares, 'rows')  127 us
    all_gather x1, blocking collectives, per_device(): lax.all_gather(values_own, 'rows', axis=0, tiled=True)  47.8 us
    all_gather x1, blocking collectives, per_device(): lax.all_gather(keys_own, 'rows', axis=0, tiled=True)  47.5 us
  transfers between devices with their start and end apart: 7, of which 7 were waited for; matrix products, arithmetic and copies ran while one was open for 0% of the time, Pallas kernels for 0%

commit v1 on v0

--- a/solution.py
+++ b/solution.py
@@ -32,21 +32,23 @@
     return lax.psum(partial_value, "tensor")
 
 
-def row_scale(squares):
-    summed = lax.psum(squares, "rows")
+def row_scale(summed):
     return lax.rsqrt(summed / D + EPSILON)
 
 
-def head_terms(normed, matrices):
-    return lax.psum_scatter(
-        jnp.concatenate(
-            [jnp.dot(normed, matrix, preferred_element_type=jnp.float32) for matrix in matrices],
-            axis=1,
-        ),
-        "rows",
-        scatter_dimension=0,
-        tiled=True,
-    )
+def head_terms(normed, matrices, squares, groups):
+    partial = jnp.concatenate(
+        [jnp.dot(normed, matrix, preferred_element_type=jnp.float32) for matrix in matrices],
+        axis=1,
+    )
+    tokens, cols = partial.shape
+    own = tokens // groups
+    payload = jnp.concatenate(
+        [partial.reshape(groups, own * cols), squares.reshape(groups, own)], axis=1
+    ).reshape(groups, 8, (own * cols + own) // 8)
+    summed = lax.psum_scatter(payload, "rows", scatter_dimension=0, tiled=True)
+    summed = summed.reshape(own * cols + own)
+    return summed[: own * cols].reshape(own, cols), summed[own * cols :]
 
 
 def head_mix(attended, matrix):
@@ -92,12 +94,17 @@
     local_ids = token_ids.reshape(token_count) - lax.axis_index("tensor") * vocab_part
     inside = (local_ids >= 0) & (local_ids < vocab_part)
     picked = jnp.take(embed_table, jnp.clip(local_ids, 0, vocab_part - 1), axis=0)
-    picked = jnp.where(inside[:, None], picked.astype(jnp.float32), 0.0)
-    embedded = width_total(picked)
-    dec_scale = row_scale(jnp.sum(embedded * embedded, axis=1))
+    picked = jnp.where(inside[:, None], picked, jnp.zeros_like(picked))
+    embedded = width_total(picked).astype(jnp.float32)
+    row_groups = token_count // own_tokens
     normed = (embedded * decode_gain[None, :]).astype(jnp.bfloat16)
-    projected = head_terms(normed, (decode_query, decode_key, decode_value))
-    projected = projected * lax.dynamic_slice_in_dim(dec_scale, row_first, own_tokens, 0)[:, None]
+    projected, dec_squares = head_terms(
+        normed,
+        (decode_query, decode_key, decode_value),
+        jnp.sum(embedded * embedded, axis=1),
+        row_groups,
+    )
+    projected = projected * row_scale(dec_squares)[:, None]
     positions = (cache_lengths[:, None] + step_ids[None, :]).reshape(own_tokens, 1)
     queries = rotate(
         projected[:, :query_cols].reshape(own_tokens, local_heads, HEAD_DIM), positions
@@ -142,7 +149,6 @@
     partial_value = head_mix(attended, decode_out)
     summary = (embedded + width_total(partial_value)).astype(jnp.bfloat16)
     summary_wide = summary.astype(jnp.float32)
-    red_scale = row_scale(jnp.sum(summary_wide * summary_wide, axis=1))
     normed_red = (summary_wide * reduce_gain[None, :]).astype(jnp.bfloat16)
     passage_index = jnp.arange(passage_count, dtype=jnp.int32)
     earlier = jnp.sum(
@@ -155,8 +161,13 @@
     doc_positions = (earlier[:, None] * step_count + step_ids[None, :]).reshape(token_count, 1)
     doc_tokens = (doc_ids[:, None] + jnp.zeros_like(step_ids)[None, :]).reshape(token_count)
     own_positions = lax.dynamic_slice_in_dim(doc_positions, row_first, own_tokens, 0)
-    own_scale = lax.dynamic_slice_in_dim(red_scale, row_first, own_tokens, 0)[:, None]
-    projected = head_terms(normed_red, (reduce_query, reduce_key, reduce_value)) * own_scale
+    projected, red_squares = head_terms(
+        normed_red,
+        (reduce_query, reduce_key, reduce_value),
+        jnp.sum(summary_wide * summary_wide, axis=1),
+        row_groups,
+    )
+    projected = projected * row_scale(red_squares)[:, None]
     queries_red = rotate(
         projected[:, :query_cols].reshape(own_tokens, local_heads, HEAD_DIM), own_positions
     ).astype(jnp.bfloat16)
@@ -169,10 +180,10 @@
         .reshape(own_tokens, kv_cols)
     )
     values_own = projected[:, query_cols + kv_cols :].astype(jnp.bfloat16)
-    keys_red, values_red = (
-        lax.all_gather(keys_own, "rows", axis=0, tiled=True),
-        lax.all_gather(values_own, "rows", axis=0, tiled=True),
-    )
+    kv_red = lax.all_gather(
+        jnp.concatenate([keys_own, values_own], axis=1), "rows", axis=0, tiled=True
+    )
+    keys_red, values_red = kv_red[:, :kv_cols], kv_red[:, kv_cols:]
     queries_red = queries_red.reshape(own_tokens, local_kv, group_size, HEAD_DIM)
     keys_red = keys_red.reshape(token_count, local_kv, HEAD_DIM)
     values_red = values_red.reshape(token_count, local_kv, HEAD_DIM)

time: 967 us -> 928 us (0.960)
  blocking collectives: 222 us -> 47.8 us
  waiting for transfers between devices: 677 us -> 774 us
  local copies, waits for them, and re-layouts: 21.6 us -> 49.3 us
    unnamed x7 -> x9, waiting for transfers between devices: 0.11 us -> 420 us
    reduce_scatter x2 -> x0, waiting for transfers between devices: 322 us -> none  [head_terms(): lax.psum_scatter(jnp.concatenate([jnp.dot(normed, matrix, preferred_eleme...]
    psum x2 -> x0, blocking collectives: 127 us -> none  [row_scale(): summed = lax.psum(squares, 'rows')]
    all_gather x2 -> x1, blocking collectives: 95.3 us -> 47.8 us  [per_device(): lax.all_gather(jnp.concatenate([keys_own, values_own], axis=1), 'rows', a...]
    reshape x0 -> x10, local copies, waits for them, and re-layouts: none -> 26.9 us  [the longest x2 13.5 us: head_terms(): payload = jnp.concatenate([partial.reshape(groups, own * cols), squares.r...]
    concatenate x0 -> x2, local copies, waits for them, and re-layouts: none -> 11.8 us  [head_terms(): jnp.concatenate([jnp.dot(normed, matrix, preferred_element_type=jnp.float...]
    unnamed x32 -> x52, local copies, waits for them, and re-layouts: 13.9 us -> 3.06 us
    concatenate x0 -> x3, other arithmetic: none -> 10.5 us  [the longest x2 10.4 us: head_terms(): jnp.concatenate([partial.reshape(groups, own * cols), squares.reshape(gro...]
where the time goes in v1:
time: 928 us; the launch traced here: 927 us
  waiting for transfers between devices  774 us (83%)
  local copies, waits for them, and re-layouts  49.3 us (5%)
  blocking collectives  47.8 us (5%)
  other arithmetic  27.3 us (3%)
  between operations  14 us (2%)
  matrix products  13.9 us (1%)
    unnamed x9, waiting for transfers between devices  420 us
    psum x3, waiting for transfers between devices, width_total(): return lax.psum(partial_value, 'tensor')  201 us
    all_gather x2, waiting for transfers between devices, head_mix(): lax.all_gather(attended, 'rows', axis=0, tiled=True)  153 us
    all_gather x1, blocking collectives, per_device(): lax.all_gather(jnp.concatenate([keys_own, values_own], axis=1), 'rows', a...  47.8 us
  transfers between devices with their start and end apart: 7, of which 7 were waited for; matrix products, arithmetic and copies ran while one was open for 0% of the time, Pallas kernels for 0%

profile of v1, /device:TPU:8, one launch (start us, length us, event | category | flops | bytes accessed | tf_op | source)
XLA Modules:
  0.0 927.0 jit_solution(14804765056638584329)
XLA Ops:
  8.8 6.2 gather_fusion
  16.3 69.0 %all-reduce.6.cloned.1.call-done = bf16[1024,256]{1,0:T(8,128)(2,1)} async-done(((bf16[1024,256]{1,0:T(8,128)(2,1)}), bf16[1024,256]{1,0:T(8,128)(2,1)}) %all-reduce.6.cloned.1.call-update) | async-done | bytes 524304 | tf_op jit(solution)/shard_map/psum | solution.py:32
  85.3 2.0 fusion.41
  88.0 2.8 pad_maximum_fusion.2
  90.8 5.9 copy.36
  96.7 5.6 reshape.597
  102.5 5.2 pad_maximum_fusion
  107.7 6.8 reshape.599
  116.9 209.4 %reduce-scatter.7.cloned.1.call-done = f32[1,8,5124]{2,1,0:T(8,128)} async-done(((f32[32,8,5124]{2,1,0:T(8,128)}), f32[1,8,5124]{2,1,0:T(8,128)}) %reduce-scatter.7.cloned.1.call-update) | async-done | bytes 163984
  333.5 76.0 %all-gather.3.cloned.1.call-done = bf16[1024,1024]{1,0:T(8,128)(2,1)} async-done(((bf16[32,1024]{1,0:T(8,128)(2,1)}), bf16[1024,1024]{1,0:T(8,128)(2,1)}) %all-gather.3.cloned.1.call-update) | async-done | bytes 2097168 | tf_op jit(solution)/shard_map/all_gather | solution.py:56
  409.5 3.3 fusion.84
  413.0 66.1 %all-reduce.8.cloned.1.call-done = f32[1024,256]{1,0:T(8,128)} async-done(((f32[1024,256]{1,0:T(8,128)}), f32[1024,256]{1,0:T(8,128)}) %all-reduce.8.cloned.1.call-update) | async-done | bytes 1048592 | tf_op jit(solution)/shard_map/psum | solution.py:32
  479.1 1.4 fusion.25
  482.1 2.9 pad_maximum_fusion.3
  485.1 5.9 copy.37
  491.0 5.6 reshape.607
  496.6 5.2 pad_maximum_fusion.1
  501.8 6.8 reshape.609
  509.6 211.0 %reduce-scatter.9.cloned.1.call-done = f32[1,8,5124]{2,1,0:T(8,128)} async-done(((f32[32,8,5124]{2,1,0:T(8,128)}), f32[1,8,5124]{2,1,0:T(8,128)}) %reduce-scatter.9.cloned.1.call-update) | async-done | bytes 163984
  722.1 47.8 %all_gather.10 = bf16[1024,256]{1,0:T(8,128)(2,1)S(1)} all-gather(bf16[32,256]{1,0:T(8,128)(2,1)S(1)} %pad_maximum_fusion.5), channel_id=1, replica_groups=mesh['rows'=32,'tensor'=8] {'rows'}, dimensions={0}, use_global_device_ids=true | all-gather | bytes 540672 | tf_op jit(solution)/shard_map/all_gather | solution.py:183
  771.9 76.5 %all-gather.5.cloned.1.call-done = bf16[1024,1024]{1,0:T(8,128)(2,1)} async-done(((bf16[32,1024]{1,0:T(8,128)(2,1)}), bf16[1024,1024]{1,0:T(8,128)(2,1)}) %all-gather.5.cloned.1.call-update) | async-done | bytes 2097168 | tf_op jit(solution)/shard_map/all_gather | solution.py:56
  848.4 3.4 fusion.85
  851.8 66.3 %all-reduce.10.cloned.1.call-done = f32[1024,256]{1,0:T(8,128)} async-done(((f32[1024,256]{1,0:T(8,128)}), f32[1024,256]{1,0:T(8,128)}) %all-reduce.10.cloned.1.call-update) | async-done | bytes 1048592 | tf_op jit(solution)/shard_map/psum | solution.py:32
  918.1 2.1 fusion.26
  (133 shorter events, 20.1 us)
Async XLA Ops:
  6.5 323.3 %copy-start = (bf16[8,1280,128]{2,1,0:T(8,128)(2,1)S(1)}, bf16[8,1280,128]{2,1,0:T(8,128)(2,1)}, u32[]{:S(2)}) copy-start(bf16[8,1280,128]{2,1,0:T(8,128)(2,1)} %param.20) | copy-start | bytes 7864324
  6.5 78.8 %copy-start.10 = (f32[256]{0:T(256)S(1)}, f32[256]{0:T(256)}, u32[]{:S(2)}) copy-start(f32[256]{0:T(256)} %param.22) | copy-start | bytes 3076
  6.5 78.8 %all-reduce.6.cloned.1.call-start = ((), (), s32[]{:S(2)}) async-start(), calls=%async_computation.2 | async-start | bytes 1048576 | tf_op jit(solution)/shard_map/psum | solution.py:32
  16.2 71.1 %copy-start.6 = (bf16[256,128]{1,0:T(8,128)(2,1)S(1)}, bf16[256,128]{1,0:T(8,128)(2,1)}, u32[]{:S(2)}) copy-start(bf16[256,128]{1,0:T(8,128)(2,1)} %param.25) | copy-start | bytes 196612
  16.2 71.5 %copy-start.7 = (bf16[256,128]{1,0:T(8,128)(2,1)S(1)}, bf16[256,128]{1,0:T(8,128)(2,1)}, u32[]{:S(2)}) copy-start(bf16[256,128]{1,0:T(8,128)(2,1)} %param.24) | copy-start | bytes 196612
  16.2 310.1 %reduce-scatter.7.cloned.1.call-start = ((), (), s32[]{:S(2)}) async-start(), calls=%async_computation.7 | async-start | bytes 5541888
  85.3 2.0 copy-start.2
  114.5 1.1 copy-start.19
  114.5 295.0 %all-gather.3.cloned.1.call-start = ((), (), s32[]{:S(2)}) async-start(), calls=%async_computation.3 | async-start | bytes 2162688 | tf_op jit(solution)/shard_map/all_gather | solution.py:56
  327.9 3.1 copy-start.22
  327.9 4.2 copy-start.20
  331.9 77.6 %copy-start.21 = (bf16[1024,256]{1,0:T(8,128)(2,1)S(1)}, bf16[1024,256]{1,0:T(8,128)(2,1)}, u32[]{:S(2)}) copy-start(bf16[1024,256]{1,0:T(8,128)(2,1)} %param.26) | copy-start | bytes 1572868
  333.4 147.1 %copy-start.5 = (bf16[256,1024]{1,0:T(8,128)(2,1)S(1)}, bf16[256,1024]{1,0:T(8,128)(2,1)}, u32[]{:S(2)}) copy-start(bf16[256,1024]{1,0:T(8,128)(2,1)} %param.28) | copy-start | bytes 1572868
  333.4 147.1 %copy-start.11 = (f32[256]{0:T(256)S(1)}, f32[256]{0:T(256)}, u32[]{:S(2)}) copy-start(f32[256]{0:T(256)} %param.27) | copy-start | bytes 3076
  333.4 145.7 %all-reduce.8.cloned.1.call-start = ((), (), s32[]{:S(2)}) async-start(), calls=%async_computation.4 | async-start | bytes 2097152 | tf_op jit(solution)/shard_map/psum | solution.py:32
  412.8 307.8 %reduce-scatter.9.cloned.1.call-start = ((), (), s32[]{:S(2)}) async-start(), calls=%async_computation.8 | async-start | bytes 5541888
  480.5 1.3 copy-start.3
  480.6 1.2 copy-start.9
  508.6 213.3 %copy-start.15 = (f32[64]{0:T(128)S(1)}, f32[64]{0:T(128)}, u32[]{:S(2)}) copy-start(f32[64]{0:T(128)} %copy-done.14) | copy-start | bytes 772
  508.6 213.3 %copy-start.18 = (f32[32]{0:T(128)S(1)}, f32[32]{0:T(128)}, u32[]{:S(2)}) copy-start(f32[32]{0:T(128)} %copy-done.17) | copy-start | bytes 388
  508.6 339.8 %all-gather.5.cloned.1.call-start = ((), (), s32[]{:S(2)}) async-start(), calls=%async_computation.5 | async-start | bytes 2162688 | tf_op jit(solution)/shard_map/all_gather | solution.py:56
  771.1 146.9 %copy-start.4 = (bf16[1024,256]{1,0:T(8,128)(2,1)S(1)}, bf16[1024,256]{1,0:T(8,128)(2,1)}, u32[]{:S(2)}) copy-start(bf16[1024,256]{1,0:T(8,128)(2,1)} %copy-done.3) | copy-start | bytes 1572868
  771.8 148.4 %copy-start.1 = (bf16[8,1280,128]{2,1,0:T(8,128)(2,1)S(1)}, bf16[8,1280,128]{2,1,0:T(8,128)(2,1)}, u32[]{:S(2)}) copy-start(bf16[8,1280,128]{2,1,0:T(8,128)(2,1)} %param.20) | copy-start | bytes 7864324
  771.8 146.2 %all-reduce.10.cloned.1.call-start = ((), (), s32[]{:S(2)}) async-start(), calls=%async_computation.6 | async-start | bytes 2097152 | tf_op jit(solution)/shard_map/psum | solution.py:32
  (6 other events, 4.6 us)
Sparse Core Ops, SparseCore 0:
  16.3 68.9 all-reduce.5
  114.6 211.6 reduce-scatter.6
  333.5 75.9 all-gather.2
  412.9 66.1 all-reduce.7
  508.7 211.8 reduce-scatter.8
  771.9 76.3 all-gather.4
  851.9 66.1 all-reduce.9
